TPU v7x, 32 devices: a whole 2x2x4 slice. The times are simulated.
32 devices in a mesh: wide: 8 (over y, x, core), narrow: 4 (over z).
Axes of the slice: x: 2, y: 2, z: 4, core: 2. Of those that a mesh axis runs over, the one named last changes fastest.
Arguments:
- tokens: float32 [4488, 768], P('wide'), may hold values from -6 to 6
- region: int32 [4488], P('wide'), may hold values from 0 to 59, as said below
- order_rank: int32 [4488], P('wide'), may hold values from 0 to 559, as said below
- box_coords: int32 [2, 4488], P(None, 'wide'), may hold values from 0 to 127
- w_query: float32 [768, 768], P(None, 'narrow'), may hold values from -0.21875 to 0.21875
- b_query: float32 [768], P('narrow'), may hold values from -3 to 3
- w_key: float32 [768, 768], P(None, 'narrow'), may hold values from -0.21875 to 0.21875
- w_value: float32 [768, 768], P(None, 'narrow'), may hold values from -0.21875 to 0.21875
- b_value: float32 [768], P('narrow'), may hold values from -0.18 to 0.18
- w_out: float32 [768, 768], P('narrow'), may hold values from -2 to 2
- b_out: float32 [768], replicated, may hold values from -2 to 2
- ln1_gain: float32 [768], replicated, may hold values from 0.1 to 1.9
- ln1_bias: float32 [768], replicated, may hold values from -2 to 2
- w_in: float32 [768, 3072], P(None, 'narrow'), may hold values from -0.21875 to 0.21875
- b_in: float32 [3072], P('narrow'), may hold values from -2 to 2
- w_down: float32 [3072, 768], P('narrow'), may hold values from -0.109375 to 0.109375
- b_down: float32 [768], replicated, may hold values from -2 to 2
- ln2_gain: float32 [768], replicated, may hold values from 0.1 to 1.9
- ln2_bias: float32 [768], replicated, may hold values from -2 to 2
- rel_order: float32 [12, 32], P('narrow'), may hold values from -3 to 3
- rel_x: float32 [12, 64], P('narrow'), may hold values from -3 to 3
- rel_y: float32 [12, 64], P('narrow'), may hold values from -3 to 3
- cotangent: float32 [4488, 768], P('wide'), may hold values from -6 to 6
Outputs:
- output: float32 [4488, 768], P('wide')
- grad_input: float32 [4488, 768], P('wide')
- grad_w_query: float32 [768, 768], P(None, 'narrow')
- grad_b_query: float32 [768], P('narrow')
- grad_w_key: float32 [768, 768], P(None, 'narrow')
- grad_w_value: float32 [768, 768], P(None, 'narrow')
- grad_b_value: float32 [768], P('narrow')
- grad_w_out: float32 [768, 768], P('narrow')
- grad_b_out: float32 [768], replicated
- grad_ln1_gain: float32 [768], replicated
- grad_ln1_bias: float32 [768], replicated
- grad_w_in: float32 [768, 3072], P(None, 'narrow')
- grad_b_in: float32 [3072], P('narrow')
- grad_w_down: float32 [3072, 768], P('narrow')
- grad_b_down: float32 [768], replicated
- grad_ln2_gain: float32 [768], replicated
- grad_ln2_bias: float32 [768], replicated
- grad_rel_order: float32 [12, 32], P('narrow')
- grad_rel_x: float32 [12, 64], P('narrow')
- grad_rel_y: float32 [12, 64], P('narrow')
Inputs may be any that keep to these rules, and one draw needn't show every extreme that they name: Each page's region ids take every value from 0 to its region count minus 1; region counts run from 2 to min(60, 561), and one page has the most. `order_rank`: within each region of a page the ranks are 0, 1, and so on up to its size minus 1, each once; no region holds more than 560 tokens, and one page has a region of exactly 560 tokens.
All inputs are finite; a program needn't handle non-finite values.
Results may differ from a plain program's by a relative error of at most 0.015.
The roundings to bfloat16 on the way count: a program that leaves them out, or rounds other values in their place, can miss the bound.
Values sent between devices are 32-bit elements; how exact they have to be, the bound alone decides.
A program may use at most 128 MiB of HBM per device.

v0:
```python
import functools
import math

import jax
import jax.numpy as jnp
import numpy as np
from jax import lax
from jax.experimental import pallas as pl
from jax.experimental.pallas import tpu as pltpu
from jax.sharding import PartitionSpec as P

HEAD_DIM = 64
BINS1 = 32
BINS2 = 64
MAX_ORDER = 128
MAX_LAYOUT = 256
PAGE = 561


HIGHEST = lax.Precision.HIGHEST
EPSILON = 1e-05
SCORE_SCALE = 0.125

def bucket_steps(bins, reach):
    halfway = bins // 2
    exact = halfway // 2
    steps = []
    for level in range(1, halfway):
        if level < exact:
            steps.append(level)
        else:
            found = reach + 1
            for count in range(exact, reach + 2):
                value = exact + int(
                    math.log(count / exact) / math.log(reach / exact) * (halfway - exact)
                )
                if min(value, halfway - 1) >= level:
                    found = count
                    break
            steps.append(found)
    return steps


MESH = pl.DeviceIdType.MESH
BLOCK = 128
PC = 32
END_PC = 32
SENT = -(-PAGE // 8) * 8
LAG = 4


def erf_of(x):
    x = jnp.clip(x, -3.832506856900711, 3.832506856900711)
    s = x * x
    top = -2.72614225801306e-10
    for term in (2.77068142495902e-08, -2.10102402082508e-06, -5.69250639462346e-05,
                 -7.34990630326855e-04, -2.95459980854025e-03, -1.60960333262415e-02):
        top = top * s + term
    low = -1.45660718464996e-05
    for term in (-2.13374055278905e-04, -1.68282697438203e-03, -7.37332916720468e-03,
                 -1.42647390514189e-02):
        low = low * s + term
    return x * top / low


def normal_cdf(x):
    return 0.5 + 0.5 * erf_of(x * math.sqrt(0.5))


def centre(values):
    c = values - jnp.mean(values, axis=-1, keepdims=True)
    r = lax.rsqrt(jnp.mean(c * c, axis=-1, keepdims=True) + EPSILON)
    return c * r, r


def norm_back(g, n, r, gain):
    m = g * gain
    return r * (m - jnp.mean(m, axis=-1, keepdims=True) - n * jnp.mean(m * n, axis=-1, keepdims=True))


def dot_nn(a, b):
    return lax.dot_general(a, b, (((1,), (0,)), ((), ())), preferred_element_type=jnp.float32)


def dot_nt(a, b):
    return lax.dot_general(a, b, (((1,), (1,)), ((), ())), preferred_element_type=jnp.float32)


def dot_tn(a, b):
    return lax.dot_general(a, b, (((0,), (0,)), ((), ())), preferred_element_type=jnp.float32)


class LineSum:
    def __init__(self, part, rx_in, rx_mid, tot, s_in, s_mid, r_in, r_mid):
        self.part, self.rx_in, self.rx_mid, self.tot = part, rx_in, rx_mid, tot
        self.s_in, self.s_mid, self.r_in, self.r_mid = s_in, s_mid, r_in, r_mid
        w, n = lax.axis_index("wide"), lax.axis_index("narrow")
        self.end = (n == 0) | (n == 3)
        self.mid = jnp.logical_not(self.end)
        self.side = (w, n + 1 - 2 * lax.rem(n, 2))
        self.across = (w, 3 - n)
        self.body = part.shape[0] // BLOCK * BLOCK // PC
        self.pieces = self.body + part.shape[0] % BLOCK // END_PC

    def rows(self, p):
        if not isinstance(p, int):
            return pl.ds(pl.multiple_of(p * PC, PC), PC)
        if p < self.body:
            return pl.ds(p * PC, PC)
        start = self.body * PC + (p - self.body) * END_PC
        return pl.ds(start, min(END_PC, SENT - start))

    def copy_a(self, p):
        return pltpu.make_async_remote_copy(self.part.at[self.rows(p)], self.rx_in.at[self.rows(p)],
            self.s_in.at[p], self.r_in.at[p], device_id=self.side, device_id_type=MESH)

    def copy_b(self, p):
        return pltpu.make_async_remote_copy(self.part.at[self.rows(p)], self.rx_mid.at[self.rows(p)],
            self.s_mid.at[p], self.r_mid.at[p], device_id=self.across, device_id_type=MESH)

    def copy_t(self, p):
        return pltpu.make_async_remote_copy(self.tot.at[self.rows(p)], self.tot.at[self.rows(p)],
            self.s_in.at[p], self.r_in.at[p], device_id=self.side, device_id_type=MESH)

    def signal(self):
        bar = pltpu.get_barrier_semaphore()
        pl.semaphore_signal(bar, inc=1, device_id=self.side, device_id_type=MESH)

        @pl.when(self.mid)
        def _():
            pl.semaphore_signal(bar, inc=1, device_id=self.across, device_id_type=MESH)

    def ready(self, others):
        bar = pltpu.get_barrier_semaphore()

        @pl.when(self.end)
        def _():
            pl.semaphore_wait(bar, 1 + others)

        @pl.when(self.mid)
        def _():
            pl.semaphore_wait(bar, 2 + others)

    def free_part(self, p):
        @pl.when(self.end)
        def _():
            self.copy_a(p).wait_send()

        @pl.when(self.mid)
        def _():
            self.copy_b(p).wait_send()

    def finish(self, p, first):
        self.copy_b(p).wait_recv()
        if not first:
            self.copy_t(p).wait_send()
        self.tot[self.rows(p), :] = self.part[self.rows(p), :] + self.rx_mid[self.rows(p), :]
        self.copy_t(p).start()

    def slot(self, p, order, done=None):
        @pl.when(self.end)
        def _():
            self.copy_a(p).start()

        @pl.when(self.mid)
        def _():
            self.copy_a(p).wait_recv()
            self.part[self.rows(p), :] += self.rx_in[self.rows(p), :]
            self.copy_b(p).start()

            if done is not None:
                for q in done:
                    self.finish(q, order == 0)
                return

            if isinstance(p, int):
                self.finish(p - LAG, order == 0)
                return

            @pl.when(p >= LAG)
            def _():
                self.finish(p - LAG, order == 0)

            if order > 0:
                @pl.when(p < LAG - 1)
                def _():
                    self.finish(p + self.pieces - LAG, order == 1)

                @pl.when(p == LAG - 1)
                def _():
                    self.finish(self.pieces - 1, order == 1)

    def send_end(self, p):
        @pl.when(self.end)
        def _():
            self.copy_a(p).start()

    def slot_mid(self, p, done):
        @pl.when(self.mid)
        def _():
            self.copy_a(p).wait_recv()
            self.part[self.rows(p), :] += self.rx_in[self.rows(p), :]
            self.copy_b(p).start()
            for q in done:
                self.finish(q, False)

    def last(self, pieces):
        @pl.when(self.mid)
        def _():
            for q in pieces:
                self.finish(q, False)

    def want(self, p):
        @pl.when(self.end)
        def _():
            self.copy_t(p).wait_recv()

    def drain(self):
        def one(p, c):
            self.free_part(p)

            @pl.when(self.mid)
            def _():
                self.copy_t(p).wait_send()
            return c
        lax.fori_loop(0, self.body, one, 0)
        for p in range(self.body, self.pieces):
            one(p, 0)


WIDE_ROWS = 640
ROWS = 576


def bucket_number(offset, bins, reach):
    halfway = bins // 2
    steps = bucket_steps(bins, reach)
    return (halfway if offset > 0 else 0) + sum(1 for s in steps if abs(offset) >= s)


def choose_matrix(offsets, bins, reach):
    out = np.zeros((bins, len(offsets)), np.float32)
    for place, offset in enumerate(offsets):
        out[bucket_number(offset, bins, reach), place] = 1.0
    return out


def split3(x):
    hi = x.astype(jnp.bfloat16)
    rest = x - hi.astype(jnp.float32)
    mid = rest.astype(jnp.bfloat16)
    return hi, mid, (rest - mid.astype(jnp.float32)).astype(jnp.bfloat16)


def split2(x):
    hi = x.astype(jnp.bfloat16)
    return hi, (x - hi.astype(jnp.float32)).astype(jnp.bfloat16)


def exact_dot(a, b, dims):
    return lax.dot_general(a, b, (dims, ((), ())), precision=HIGHEST, preferred_element_type=jnp.float32)


def lanes_of(h, shape):
    lane = lax.broadcasted_iota(jnp.int32, shape, 1)
    return (lane >= h * HEAD_DIM) & (lane < (h + 1) * HEAD_DIM)


def block_rows(m, n):
    return pl.ds(m * BLOCK, n) if isinstance(m, int) else pl.ds(pl.multiple_of(m * BLOCK, BLOCK), n)


def block_window(m):
    start = 512 - m * BLOCK
    return pl.ds(start if isinstance(m, int) else pl.multiple_of(start, 128), WIDE_ROWS)


class CubeSum:
    def __init__(self, ref, rx1, rx2, rx3, rxb, ssem, rsem, free, bits):
        self.ref, self.rx1, self.rx2, self.rx3, self.rxb = ref, rx1, rx2, rx3, rxb
        self.ssem, self.rsem, self.free = ssem, rsem, free
        w, n = lax.axis_index("wide"), lax.axis_index("narrow")
        self.bit = [lax.rem(lax.div(w, 2 ** i), 2) for i in range(bits)]
        self.to = [(w + 2 ** i * (1 - 2 * self.bit[i]), n) for i in range(bits)]
        self.rows = ref.shape[0]
        half = self.rows // 2
        self.half, self.stream, self.eighth, self.piece = half, half // 2, half // 4, half // 8
        self.own = self.bit[0] * half
        self.axes = ((1, 2), (2, 1))
        self.extra = range(3, bits)

    def at(self, start, size):
        return pl.ds(pl.multiple_of(start, self.piece), size)

    def base1(self, s, other):
        b = self.bit[self.axes[s][0]]
        b = 1 - b if other else b
        return self.own + s * self.stream + b * self.eighth

    def base2(self, s, other):
        b = self.bit[self.axes[s][1]]
        b = 1 - b if other else b
        return self.base1(s, False) + b * self.piece

    def copy(self, src, dst, i, axis):
        return pltpu.make_async_remote_copy(src, dst, self.ssem.at[i], self.rsem.at[i], device_id=self.to[axis],
                                            device_id_type=MESH)

    def core_out(self):
        return self.copy(self.ref.at[self.at((1 - self.bit[0]) * self.half, self.half)], self.rx1, 0, 0)

    def first(self, s):
        return self.copy(self.ref.at[self.at(self.base1(s, True), self.eighth)], self.rx2[s], 1 + s, self.axes[s][0])

    def second(self, s):
        return self.copy(self.ref.at[self.at(self.base2(s, True), self.piece)], self.rx3[s], 3 + s, self.axes[s][1])

    def back2(self, s):
        r = self.at(self.base2(s, False), self.piece)
        return self.copy(self.ref.at[r], self.rxb[s], 5 + s, self.axes[s][1])

    def back1(self, s):
        r = self.at(self.base1(s, False), self.eighth)
        return self.copy(self.ref.at[r], self.ref.at[r], 7 + s, self.axes[s][0])

    def core_back(self):
        r = self.at(self.own, self.half)
        return self.copy(self.ref.at[r], self.ref.at[r], 9, 0)

    def spare(self, e, s):
        return pl.ds((2 * (e - 3) + s) * self.piece, self.piece)

    def more(self, e, s):
        return self.copy(self.ref.at[self.at(self.base2(s, False), self.piece)], self.rx1.at[self.spare(e, s)],
                         10 + 2 * (e - 3) + s, e)

    def release(self, i, axis):
        pl.semaphore_signal(self.free.at[i], inc=1, device_id=self.to[axis], device_id_type=MESH)

    def step(self, i):
        if i == 0:
            self.core_out().start()
        if i == 1:
            self.core_out().wait_recv()
            self.ref[self.at(self.own, self.half), :] += self.rx1[...]
            for s in range(2):
                self.first(s).start()
            self.core_out().wait_send()
            self.release(0, 0)
            for e in self.extra:
                self.release(e, e)
        if i == 2:
            for s in range(2):
                self.first(s).wait()
                self.release(1 + s, self.axes[s][0])
                self.ref[self.at(self.base1(s, False), self.eighth), :] += self.rx2[s][...]
                self.second(s).start()
        if i == 3:
            for s in range(2):
                self.second(s).wait()
                self.ref[self.at(self.base2(s, False), self.piece), :] += self.rx3[s][...]
            for e in self.extra:
                pl.semaphore_wait(self.free.at[e], 1)
                for s in range(2):
                    self.more(e, s).start()
                for s in range(2):
                    self.more(e, s).wait()
                    self.ref[self.at(self.base2(s, False), self.piece), :] += self.rx1[self.spare(e, s), :]
            for s in range(2):
                self.back2(s).start()
        if i == 4:
            for s in range(2):
                self.back2(s).wait_recv()
                self.ref[self.at(self.base2(s, True), self.piece), :] = self.rxb[s][...]
                pl.semaphore_wait(self.free.at[1 + s], 1)
                self.back1(s).start()
        if i == 5:
            for s in range(2):
                self.back1(s).wait_recv()
            pl.semaphore_wait(self.free.at[0], 1)
            self.core_back().start()
        if i == 6:
            self.core_back().wait()
            for s in range(2):
                self.back2(s).wait_send()
                self.back1(s).wait_send()


def layer_kernel(bits, tok_h, cot_h, wq_h, wk_h, wv_h, wo_h, wi_h, wd_h, reg, rank, box, bq, bv, bo_r, g1_r, b1_r, bi_r, bd_r, g2_r, b2_r,
                 to, tx, ty, so, sxy, sgo, sgxy,
                 out, gin, gat, gwi, gwd, sm,
                 part, rx_in, rx_mid, tot, res, cotp, hid, pre, act, gff, hlow, gpre, low, perm,
                 q_s, k_s, v_s, prob, att, ob, obf, pairs, ob4, split_s, base, ga, gt, qt, dkt, dvt, dqkv, gacc, trow,
                 ws, wo, wi, wd, outp, rows_s, vec_s, rx1, rx2, rx3, rxb, rxs,
                 s_in, s_mid, r_in, r_mid, cs, cr, cf, ss, sr, ls):
    f32, bf = jnp.float32, jnp.bfloat16
    n = PAGE
    width = wo_h.shape[0]
    heads = to.shape[0]
    block_pieces = BLOCK // PC
    dq, dk, dv = (dqkv.at[i] for i in range(3))
    tail_pieces = ROWS % BLOCK // END_PC

    def pieces_of(m, rows):
        return [m * block_pieces + j for j in range(block_pieces if rows == BLOCK else tail_pieces)]
    line = LineSum(part, rx_in, rx_mid, tot, s_in, s_mid, r_in, r_mid)
    pieces = line.pieces
    closing = {pieces - 2: [pieces - 6, pieces - 5], pieces - 1: [pieces - 4, pieces - 3]}
    rest1, rest2, rest3, restb = pre.at[pl.ds(0, 384)], pre.at[pl.ds(384, 192)], cotp.at[pl.ds(0, 96)], cotp.at[pl.ds(96, 96)]
    cube = [CubeSum(gwi, rx1.at[0], [rx2.at[0, s] for s in range(2)], [rx3.at[0, s] for s in range(2)],
                    [rxb.at[0, s] for s in range(2)], cs.at[0], cr.at[0], cf.at[0], bits),
            CubeSum(gwd, rx1.at[1], [rx2.at[1, s] for s in range(2)], [rx3.at[1, s] for s in range(2)],
                    [rxb.at[1, s] for s in range(2)], cs.at[1], cr.at[1], cf.at[1], bits),
            CubeSum(gat, rest1, [pre.at[pl.ds(384 + 96 * s, 96)] for s in range(2)],
                    [cotp.at[pl.ds(48 * s, 48)] for s in range(2)],
                    [cotp.at[pl.ds(96 + 48 * s, 48)] for s in range(2)], cs.at[2], cr.at[2], cf.at[2], bits)]

    def load(i, src, dst):
        return pltpu.make_async_copy(src, dst, ls.at[i])
    loads = [load(0, tok_h, out)]
    loads += [load(1 + i, src, gat.at[pl.ds(i * width, width)]) for i, src in enumerate((wq_h, wk_h, wv_h, wo_h))]
    loads += [load(5, wi_h, gwi), load(6, wd_h, gwd), load(7, cot_h, gin)]
    for c in loads:
        c.start()
    bar = pltpu.get_barrier_semaphore()
    for peer in cube[0].to:
        pl.semaphore_signal(bar, inc=1, device_id=peer, device_id_type=MESH)
    line.signal()
    tot[SENT:ROWS, :] = jnp.zeros((ROWS - SENT, tot.shape[1]), f32)

    rows_s[...] = jnp.full(rows_s.shape, 1e4, f32)
    rows_s[0, 0:n] = reg[...].astype(f32)
    rows_s[1, 0:n] = rank[...].astype(f32)
    rows_s[2:4, 0:n] = box[...].astype(f32)
    region_row, rank_row = rows_s[0:1, :], rows_s[1:2, :]
    i0 = lax.broadcasted_iota(jnp.int32, (WIDE_ROWS, WIDE_ROWS), 0)
    i1 = lax.broadcasted_iota(jnp.int32, (WIDE_ROWS, WIDE_ROWS), 1)
    region_col = jnp.sum(jnp.where(i0 == i1, region_row, 0.0), axis=1, keepdims=True)
    place = jnp.sum(jnp.where(region_col < region_row, 1.0, 0.0), axis=0, keepdims=True) + rank_row
    perm[...] = jnp.where(i0.astype(f32) == place, 1.0, 0.0).astype(bf)
    split_s[...] = jnp.zeros_like(split_s)
    for i, vector in enumerate((bo_r, g1_r, b1_r, bi_r, bd_r, g2_r, b2_r)):
        vec_s[i, :] = vector[...]
    vec_s[7:9, :] = jnp.zeros((2, vec_s.shape[1]), f32)
    vec_s[7, 0:width] = bq[...]
    vec_s[8, 0:width] = bv[...]
    b_out, g1, b1, b_in, b_down, g2, b2 = (vec_s[i:i + 1, :] for i in range(7))

    def sort_first(source, target, first):
        split_s[0:n, :] = source[...].astype(bf)
        y = dot_nn(perm[...], split_s[...])
        if first is not None:
            first[...] = y.astype(bf)
        target[...] = y[0:ROWS, :]

    def sort_rest(source, target):
        for i in range(1, 3):
            split_s[0:n, :] = split3(source[...])[i]
            target[...] += dot_nn(perm[0:ROWS, :], split_s[...])

    loads[0].wait()
    sort_first(out, res, low)
    code = lax.broadcasted_iota(jnp.int32, (128, WIDE_ROWS), 0).astype(f32)
    for i in range(2):
        row = rows_s[2 + i:3 + i, :]
        one = dot_nt(perm[...], jnp.where(code == row, 1.0, 0.0).astype(bf)).astype(bf)
        ob[:, 128 * i:128 * (i + 1)] = one
        ob4[:, 256 * i:256 * i + 128] = one
        ob4[:, 256 * i + 128:256 * i + 256] = one
    ws[...] = jnp.zeros_like(ws)
    for i in range(3):
        loads[1 + i].wait()
        ws[i, 0:width, :] = gat[i * width:(i + 1) * width, :].astype(bf)
    q_s[...] = ((dot_nt(low[...], ws[0]) + vec_s[7:8, 0:256]).astype(bf) * SCORE_SCALE).astype(bf)
    k_s[...] = dot_nt(low[...], ws[1]).astype(bf)
    v_s[...] = (dot_nt(low[...], ws[2]) + vec_s[8:9, 0:256]).astype(bf)
    wo[...] = jnp.zeros_like(wo)
    loads[4].wait()
    wo[0:width, :] = gat[3 * width:4 * width, :].astype(bf)
    row_o = exact_dot(to[...], so[...], ((1,), (0,)))
    row_xy = (exact_dot(tx[...], sxy[...], ((1,), (0,))), exact_dot(ty[...], sxy[...], ((1,), (0,))))
    for h in range(heads):
        base[h] = pltpu.roll(jnp.broadcast_to(row_o[h:h + 1, :], (128, 1280)), 0, 1, stride=1, stride_axis=0)
        for i in range(2):
            table = pltpu.roll(jnp.broadcast_to(row_xy[i][h:h + 1, :], (128, 256)), 0, 1, stride=1, stride_axis=0)
            pairs[h, i] = jnp.concatenate(split2(table[:, 0:128]), axis=1)
    line.ready(bits)

    def blocks(body, start=0):
        full = ROWS // BLOCK

        def step(m, carry):
            body(m, BLOCK)
            return carry
        lax.fori_loop(start, full, step, 0)
        if ROWS % BLOCK:
            body(full, ROWS % BLOCK)

    def sends(m, rows, order):
        if rows == BLOCK:
            def one_slot(j, carry):
                line.slot(m * block_pieces + j, order)
                return carry
            lax.fori_loop(0, block_pieces, one_slot, 0)
            return
        for p in pieces_of(m, rows):
            line.slot(p, order, closing[p] if order == 2 and isinstance(p, int) else None)

    def attend(m, rows):
        r = block_rows(m, rows)
        mixed = None
        for h in range(heads):
            qh = jnp.where(lanes_of(h, (rows, 256)), q_s[r, :], jnp.zeros((), bf))
            bias = jnp.concatenate([dot_nn(ob[r, 128 * i:128 * (i + 1)], pairs[h, i]).astype(bf) for i in range(2)], axis=1)
            s = dot_nt(qh, k_s[...]) + dot_nt(bias, ob4[...]) + base[h, 0:rows, block_window(m)]
            s = jnp.where(lax.broadcasted_iota(jnp.int32, s.shape, 1) < n, s, -1e30)
            e = jnp.exp(s - jnp.max(s, axis=1, keepdims=True))
            p = e / jnp.sum(e, axis=1, keepdims=True)
            prob[h, r, :] = p
            pv = dot_nn(p.astype(bf), v_s[...])
            mixed = pv if h == 0 else jnp.where(lanes_of(h, (rows, 256)), pv, mixed)
        mixed = mixed.astype(bf)
        att[r, :] = mixed
        part[r, :] = dot_nn(mixed, wo[...])
        sends(m, rows, 0)
        if rows == BLOCK:
            pl.when(m == 1)(early_one)
            pl.when(m == 2)(early_two)

    def early_one():
        sort_rest(out, res)

    def early_two():
        loads[5].wait()
        wi[...] = gwi[...].astype(bf)
        loads[6].wait()
        wd[...] = gwd[...].astype(bf)
        sm[...] = jnp.zeros_like(sm)
    blocks(attend)

    def open_block(m, rows):
        for p in pieces_of(m, rows):
            line.want(p)
        for p in pieces_of(m, rows):
            line.free_part(p)

    def forward(m, rows):
        r = block_rows(m, rows)
        open_block(m, rows)
        one = res[r, :] + (tot[r, :] + b_out)
        res[r, :] = one
        c, _ = centre(one)
        hidden = c * g1 + b1
        hid[r, :] = hidden
        hl = hidden.astype(bf)
        hlow[r, :] = hl
        u = dot_nn(hl, wi[...]) + b_in
        pre[r, :] = u
        a = (u * normal_cdf(u)).astype(bf)
        act[r, :] = a
        part[r, :] = dot_nn(a, wd[...])
        sends(m, rows, 1)
        if rows == BLOCK:
            pl.when(m == 0)(late_one)
            pl.when(m == 1)(late_two)
            pl.when(m == 2)(late_three)

    def late_one():
        loads[7].wait()
        sort_first(gin, cotp, None)

    def late_two():
        sort_rest(gin, cotp)

    def late_three():
        for i in range(2):
            row = rows_s[2 + i:3 + i, :]
            obf[:, 128 * i:128 * (i + 1)] = dot_nt(perm[...], jnp.where(127.0 - code == row, 1.0, 0.0).astype(bf)).astype(bf)
        outp[...] = jnp.zeros_like(outp)
        qt[...] = jnp.transpose(q_s[...])
        dkt[...] = jnp.zeros_like(dkt)
        dvt[...] = jnp.zeros_like(dvt)
        base[...] = jnp.zeros_like(base)
        gacc[...] = jnp.zeros_like(gacc)
        ga[...] = jnp.zeros_like(ga)
        dq[...] = jnp.zeros_like(dq)
        gat[3 * width:4 * width, :] = jnp.zeros((width, gat.shape[1]), f32)
    blocks(forward)

    def add_row(i, value):
        sm[i:i + 1, :] += jnp.sum(value, axis=0, keepdims=True)

    def put_back(r, y):
        total = outp[...]
        for piece in split3(y):
            total = total + dot_tn(perm[r, :], piece)
        outp[...] = total

    def back(m, rows):
        r = block_rows(m, rows)
        open_block(m, rows)
        two = hid[r, :] + (tot[r, :] + b_down)
        c, rs = centre(two)
        g = cotp[r, :]
        add_row(0, g * c)
        add_row(1, g)
        gradient = norm_back(g, c, rs, g2)
        hid[r, :] = gradient
        gl = gradient.astype(bf)
        gff[r, :] = gl
        add_row(2, gl.astype(f32))
        slope_in = dot_nt(gl, wd[...])
        u = pre[r, :]
        slope = normal_cdf(u) + u * (jnp.exp(-0.5 * u * u) * (1.0 / math.sqrt(2.0 * math.pi)))
        gp = (slope_in * slope).astype(bf)
        gpre[r, :] = gp
        add_row(3, gp.astype(f32))
        part[r, :] = dot_nt(gp, wi[...])
        sends(m, rows, 2)
        put_back(r, c * g2 + b2)

    def attend_back(m, rows):
        r = block_rows(m, rows)
        for p in pieces_of(m, rows):
            line.want(p)
        g = hid[r, :] + tot[r, :]
        c, rs = centre(res[r, :])
        add_row(4, g * c)
        add_row(5, g)
        gradient = norm_back(g, c, rs, g1)
        hid[r, :] = gradient
        gb = gradient.astype(bf)
        add_row(6, gb.astype(f32))
        gat[3 * width:4 * width, :] += dot_tn(att[r, :], gb)[0:width, :]
        gab = dot_nt(gb, wo[...]).astype(bf)
        ga[0:rows, :] = gab
        gt[...] = jnp.transpose(ga[...])
        cols = pl.ds(pl.multiple_of(m * BLOCK, BLOCK), rows)
        query_grad = None
        for h in range(heads):
            gh = jnp.where(lanes_of(h, (rows, 256)), gab, jnp.zeros((), bf))
            dp = dot_nt(gh, v_s[...])
            p = prob[h, r, :]
            inner = jnp.sum(p * dp, axis=1, keepdims=True)
            ds = (p * (dp - inner)).astype(bf)
            dqh = dot_nn(ds, k_s[...])
            query_grad = dqh if h == 0 else jnp.where(lanes_of(h, (rows, 256)), dqh, query_grad)
            base[h, 0:rows, block_window(m)] += ds.astype(f32)
            hr = pl.ds(h * HEAD_DIM, HEAD_DIM)
            dkt[hr, :] += dot_nn(qt[hr, cols], ds)
            dvt[hr, :] += dot_nn(gt[hr, 0:rows], p.astype(bf))
            u = jnp.concatenate(split2(dot_nn(ds, ob[...])), axis=1)
            gg = dot_tn(obf[r, :], u)
            for i in range(2):
                b = 128 * i
                gacc[h, i] += gg[b:b + 128, b:b + 128] + gg[b:b + 128, 256 + b:384 + b]
        dq[r, :] = jnp.where(lax.broadcasted_iota(jnp.int32, (rows, 256), 1) < width, query_grad * SCORE_SCALE, 0.0).astype(bf)

    def back_step(m, carry):
        back(m, BLOCK)

        @pl.when(m == ROWS // BLOCK - 1)
        def _():
            attend_back(0, BLOCK)
        return carry
    lax.fori_loop(0, ROWS // BLOCK, back_step, 0)
    back(ROWS // BLOCK, ROWS % BLOCK)

    gwd[...] = dot_tn(act[...], gff[...])
    cube[1].step(0)
    gwi[...] = dot_tn(hlow[...], gpre[...])
    cube[0].step(0)
    line.last([pieces - 2, pieces - 1])

    def late_step(m, carry):
        attend_back(m, BLOCK)

        @pl.when(m == 1)
        def _():
            cube[1].step(1)

        @pl.when(m == 2)
        def _():
            cube[0].step(1)
        return carry
    lax.fori_loop(1, ROWS // BLOCK, late_step, 0)
    out[...] = outp[0:n, :]
    outp[...] = jnp.zeros_like(outp)
    attend_back(ROWS // BLOCK, ROWS % BLOCK)
    dk[...] = jnp.transpose(dkt[...]).astype(bf)
    dv[...] = jnp.transpose(dvt[...]).astype(bf)

    def produce(m, rows):
        r = block_rows(m, rows)
        for p in pieces_of(m, rows):
            line.free_part(p)
        part[r, :] = dot_nn(dq[r, :], ws[0]) + dot_nn(dk[r, :], ws[1]) + dot_nn(dv[r, :], ws[2])
        for p in pieces_of(m, rows):
            line.send_end(p)
    blocks(produce)

    def table_sums(_):
        flip = (lax.broadcasted_iota(jnp.int32, (128, 128), 0) + lax.broadcasted_iota(jnp.int32, (128, 128), 1)) == 127
        flip = jnp.where(flip, 1.0, 0.0).astype(bf)

        def one(h, carry):
            for i in range(2):
                both = jnp.concatenate([gacc[h, i], jnp.zeros((128, 128), f32)], axis=1)
                line_sum = jnp.sum(pltpu.roll(both, 0, 1, stride=1, stride_axis=0), axis=0, keepdims=True)
                trow[h, i + 1:i + 2, 0:BINS2] = exact_dot(line_sum, sgxy[...], ((1,), (1,)))
            hi, lo = split2(base[h])
            turned = dot_nn(flip, hi) + dot_nn(flip, lo)
            line_sum = jnp.sum(pltpu.roll(turned, 0, 1, stride=1, stride_axis=0), axis=0, keepdims=True)
            trow[h, 0:1, 0:BINS1] = exact_dot(line_sum, sgo[...], ((1,), (1,)))
            return carry
        lax.fori_loop(0, heads, one, 0)
        for h in range(heads):
            for i, bins in enumerate((BINS1, BINS2, BINS2)):
                sm[10 + heads * i + h:11 + heads * i + h, 0:bins] = trow[h, i:i + 1, 0:bins]

    def bias_sums(_):
        sm[8:9, 0:256] = jnp.sum(dq[...].astype(f32), axis=0, keepdims=True)
        sm[9:10, 0:256] = jnp.sum(dv[...].astype(f32), axis=0, keepdims=True)

    bit_to = cube[0].to

    def small_copy(i):
        return pltpu.make_async_remote_copy(sm, rxs.at[i], ss.at[i], sr.at[i], device_id=bit_to[i], device_id_type=MESH)

    def small_step(i):
        if i > 0:
            small_copy(i - 1).wait()
            sm[...] += rxs[i - 1]
        if i < bits:
            small_copy(i).start()

    def weight_grads():
        def one(i, carry):
            gat[pl.ds(pl.multiple_of(i * width, HEAD_DIM), width), :] = dot_tn(dqkv[i], low[...])[0:width, :]
            return carry
        lax.fori_loop(0, 3, one, 0)

    def consume(m):
        rows = min(BLOCK, ROWS - m * BLOCK)
        for p in pieces_of(m, rows):
            line.want(p)
        r = slice(m * BLOCK, m * BLOCK + rows)
        put_back(r, hid[r, :] + tot[r, :])

    jobs = {1: [(bias_sums, 0), (table_sums, 0)], 2: [], 3: [(cube[1].step, 3), (cube[0].step, 3)], 5: [], 6: [(cube[2].step, 1), (small_step, 0)], 7: [(cube[1].step, 4), (cube[0].step, 4)], 9: [(small_step, 1)], 10: [(cube[2].step, 2)], 11: [(consume, 0)], 12: [(small_step, 2)], 13: [(consume, 1)], 14: [(cube[2].step, 3)], 15: [(small_step, 3)], 16: [(cube[1].step, 5), (cube[0].step, 5)]}
    cube[1].step(2)
    cube[0].step(2)
    weight_grads()
    cube[2].step(0)
    ending = {p: [p - LAG] for p in range(LAG, pieces - 4)}
    ending.update({pieces - 4: [pieces - 8, pieces - 7], pieces - 3: [pieces - 6], pieces - 2: [pieces - 5, pieces - 4],
                   pieces - 1: [pieces - 3, pieces - 2]})
    for p in range(pieces):
        line.slot_mid(p, ending.get(p, ()))
        for job, arg in jobs.get(p, ()):
            job(arg)
    line.last([pieces - 1])
    for i in range(4, bits + 1):
        small_step(i)
    cube[2].step(4)
    consume(2)
    cube[2].step(5)
    consume(3)
    consume(4)
    for c in cube:
        c.step(6)
    gin[...] = outp[0:n, :]
    line.drain()


def layer(bits, tok, cot, wq, wk, wv, wo, wi, wd, *small_args):
    f32, bf = jnp.float32, jnp.bfloat16
    d = tok.shape[1]
    f = wi.shape[1]
    width = wo.shape[0]
    heads = small_args[12].shape[0]
    sd = jax.ShapeDtypeStruct
    W, R = WIDE_ROWS, ROWS
    pieces = R // BLOCK * BLOCK // PC + R % BLOCK // END_PC
    more = max(bits - 3, 1)
    vm, hbm = pl.BlockSpec(memory_space=pltpu.VMEM), pl.BlockSpec(memory_space=pl.ANY)
    v_ = pltpu.VMEM
    shapes = (v_((PAGE, d), f32), v_((PAGE, d), f32), v_((4 * width, d), f32), v_((d, f), f32), v_((f, d), f32), v_((24, d), f32))
    scratch = [v_((R, d), f32)] * 7 + [v_((R, f), f32), v_((R, f), bf), v_((R, d), bf), v_((R, d), bf), v_((R, f), bf)]
    scratch += [v_((W, d), bf), v_((W, W), bf)] + [v_((W, 256), bf)] * 3 + [v_((heads, R, W), f32)] + [v_((W, 256), bf)] * 3
    scratch += [v_((heads, 2, 128, 256), bf), v_((W, 512), bf), v_((W, d), bf), v_((heads, 128, 1280), f32)]
    scratch += [v_((BLOCK, 256), bf), v_((256, BLOCK), bf), v_((256, W), bf), v_((256, W), f32), v_((256, W), f32)]
    scratch += [v_((3, W, 256), bf), v_((heads, 2, 128, 128), f32), v_((heads, 8, 128), f32)]
    scratch += [v_((3, 256, d), bf), v_((256, d), bf), v_((d, f), bf), v_((f, d), bf), v_((W, d), f32), v_((8, W), f32), v_((16, d), f32)]
    scratch += [v_((2, d // 2, d), f32), v_((2, 2, d // 8, d), f32), v_((2, 2, d // 16, d), f32), v_((2, 2, d // 16, d), f32), v_((bits, 24, d), f32)]
    scratch += [pltpu.SemaphoreType.DMA((pieces,))] * 4 + [pltpu.SemaphoreType.DMA((3, 10 + 2 * more))] * 2
    scratch += [pltpu.SemaphoreType.REGULAR((3, max(bits, 3)))] + [pltpu.SemaphoreType.DMA((bits,))] * 2 + [pltpu.SemaphoreType.DMA((8,))]
    return pl.pallas_call(
        functools.partial(layer_kernel, bits), out_shape=shapes, in_specs=[hbm] * 8 + [vm] * 19, out_specs=[vm] * 6,
        scratch_shapes=scratch,
        compiler_params=pltpu.CompilerParams(collective_id=0, has_side_effects=True, vmem_limit_bytes=52 << 20),
        cost_estimate=pl.CostEstimate(flops=3 * 10 ** 10, bytes_accessed=20 << 20, transcendentals=heads * R * W),
    )(tok, cot, wq, wk, wv, wo, wi, wd, *small_args)


def finish_kernel(out_in, gin_in, gat_in, gwi_in, gwd_in, sm, out, gin, gwq, gwk, gwv, gwo, gwi, gwd, *rest):
    vectors, sem = rest[:12], rest[12]
    width = gwo.shape[0]
    heads = vectors[9].shape[0]
    pairs = [(out_in, out), (gin_in, gin), (gwi_in, gwi), (gwd_in, gwd)]
    pairs += [(gat_in.at[pl.ds(i * width, width)], g) for i, g in enumerate((gwq, gwk, gwv, gwo))]
    copies = [pltpu.make_async_copy(a, b, sem.at[i]) for i, (a, b) in enumerate(pairs)]
    for c in copies:
        c.start()
    for i in range(7):
        vectors[i][...] = sm[i, :]
    vectors[7][...] = sm[8, 0:width]
    vectors[8][...] = sm[9, 0:width]
    vectors[9][...] = sm[10:10 + heads, 0:BINS1]
    vectors[10][...] = sm[10 + heads:10 + 2 * heads, 0:BINS2]
    vectors[11][...] = sm[10 + 2 * heads:10 + 3 * heads, 0:BINS2]
    for c in copies:
        c.wait()


def finish(heads, width, out, gin, gat, gwi, gwd, sm):
    f32 = jnp.float32
    sd = jax.ShapeDtypeStruct
    d = gat.shape[1]
    like = lambda x: sd(x.shape, f32)
    shapes = (like(out), like(gin)) + (sd((width, d), f32),) * 4 + (like(gwi), like(gwd)) + (sd((d,), f32),) * 7 \
        + (sd((width,), f32),) * 2 + (sd((heads, BINS1), f32), sd((heads, BINS2), f32), sd((heads, BINS2), f32))
    vm, hbm = pl.BlockSpec(memory_space=pltpu.VMEM), pl.BlockSpec(memory_space=pl.ANY)
    return pl.pallas_call(
        finish_kernel, out_shape=shapes, in_specs=[vm] * 6, out_specs=[hbm] * 8 + [vm] * 12,
        scratch_shapes=[pltpu.SemaphoreType.DMA((8,))],
        compiler_params=pltpu.CompilerParams(vmem_limit_bytes=4 << 20),
    )(*(pltpu.with_memory_space_constraint(x, pltpu.VMEM) for x in (out, gin, gat, gwi, gwd, sm)))


def local(
    bits,
    tokens,
    region,
    order_rank,
    box_coords,
    w_query,
    b_query,
    w_key,
    w_value,
    b_value,
    w_out,
    b_out,
    ln1_gain,
    ln1_bias,
    w_in,
    b_in,
    w_down,
    b_down,
    ln2_gain,
    ln2_bias,
    rel_order,
    rel_x,
    rel_y,
    cotangent,
):
    so = choose_matrix([i - 512 if i < 1152 else i - 1792 for i in range(1280)], BINS1, MAX_ORDER)
    sxy = choose_matrix([i if i < 128 else i - 256 for i in range(256)], BINS2, MAX_LAYOUT)
    sgo = choose_matrix([i - 639 for i in range(1280)], BINS1, MAX_ORDER)
    sgxy = choose_matrix([i - 127 for i in range(256)], BINS2, MAX_LAYOUT)
    width = w_out.shape[0]
    heads = rel_order.shape[0]
    output, gin, gat, gwi, gwd, sm = layer(
        bits, tokens, cotangent, w_query.T, w_key.T, w_value.T, w_out, w_in, w_down, region, order_rank, box_coords, b_query, b_value,
        b_out, ln1_gain, ln1_bias, b_in, b_down, ln2_gain, ln2_bias, rel_order, rel_x, rel_y, so, sxy, sgo, sgxy)
    (output, gin, gwq, gwk, gwv, gwo, gwi, gwd, l2g, l2b, bd, bi, l1g, l1b, bo, gbq, gbv, ro, rx, ry) = finish(
        heads, width, output, gin, gat, gwi, gwd, sm)
    return (output, gin, gwq.T, gbq, gwk.T, gwv.T, gbv, gwo, bo, l1g, l1b, gwi, bi,
            gwd, bd, l2g, l2b, ro, rx, ry)


def solution(mesh):
    in_specs = (
        P("wide", None),
        P("wide"),
        P("wide"),
        P(None, "wide"),
        P(None, "narrow"),
        P("narrow"),
        P(None, "narrow"),
        P(None, "narrow"),
        P("narrow"),
        P("narrow", None),
        P(),
        P(),
        P(),
        P(None, "narrow"),
        P("narrow"),
        P("narrow", None),
        P(),
        P(),
        P(),
        P("narrow", None),
        P("narrow", None),
        P("narrow", None),
        P("wide", None),
    )
    out_specs = (
        P("wide", None),
        P("wide", None),
        P(None, "narrow"),
        P("narrow"),
        P(None, "narrow"),
        P(None, "narrow"),
        P("narrow"),
        P("narrow", None),
        P(),
        P(),
        P(),
        P(None, "narrow"),
        P("narrow"),
        P("narrow", None),
        P(),
        P(),
        P(),
        P("narrow", None),
        P("narrow", None),
        P("narrow", None),
    )
    bits = mesh.shape["wide"].bit_length() - 1
    return jax.shard_map(functools.partial(local, bits), mesh=mesh, in_specs=in_specs, out_specs=out_specs, check_vma=False)
```

profile of v0, /device:TPU:0, one launch (start us, length us, event | category | flops | bytes accessed | tf_op | source)
XLA Modules:
  0.0 208.5 jit_solution(3242535106935083463)
XLA Ops:
  0.7 202.9 %shard_map.410 = (f32[561,768]{1,0:T(8,128)S(1)}, f32[561,768]{1,0:T(8,128)S(1)}, f32[768,768]{1,0:T(8,128)S(1)}, f32[768,768]{1,0:T(8,128)S(1)}, f32[768,768]{1,0:T(8,128)S(1)}, /*index=5*/f32[24,768]{1,0:T(8,128)S(1)}) custom-call(f32[561,768]{1,0:T(8,128)} %tok_h.1, f32[561,768]{1,0:T(8,128)} %cot_h.1, f32[192,768]{1,0:T(8,128)} %bitcast.6, ...), custom_call_target="tpu_custom_call" | custom-call | flops 30000001024 | bytes 20971520 | tf_op jit(solution)/shard_map/pallas_call | solution.py:798
  203.6 4.7 %shard_map.411 = (f32[561,768]{1,0:T(8,128)}, f32[561,768]{1,0:T(8,128)}, f32[192,768]{1,0:T(8,128)}, f32[192,768]{1,0:T(8,128)}, f32[192,768]{1,0:T(8,128)}, /*...) custom-call(f32[561,768]{1,0:T(8,128)S(1)} %get-tuple-element.46.out, ...), custom_call_target="tpu_custom_call" | custom-call | tf_op jit(solution)/shard_map/pallas_call | solution.py:834
where the time goes:
time: 209 us; the launch traced here: 208 us
  Pallas kernels  208 us (100%)
    pallas_call x1, Pallas kernels, layer(): pl.pallas_call(functools.partial(layer_kernel, bits), out_shape=shapes, i...  203 us
    pallas_call x1, Pallas kernels, finish(): pl.pallas_call(finish_kernel, out_shape=shapes, in_specs=[vm] * 6, out_sp...  4.69 us

commit v1 on v0

--- a/solution.py
+++ b/solution.py
@@ -747,7 +747,7 @@
         r = slice(m * BLOCK, m * BLOCK + rows)
         put_back(r, hid[r, :] + tot[r, :])
 
-    jobs = {1: [(bias_sums, 0), (table_sums, 0)], 2: [], 3: [(cube[1].step, 3), (cube[0].step, 3)], 5: [], 6: [(cube[2].step, 1), (small_step, 0)], 7: [(cube[1].step, 4), (cube[0].step, 4)], 9: [(small_step, 1)], 10: [(cube[2].step, 2)], 11: [(consume, 0)], 12: [(small_step, 2)], 13: [(consume, 1)], 14: [(cube[2].step, 3)], 15: [(small_step, 3)], 16: [(cube[1].step, 5), (cube[0].step, 5)]}
+    jobs = {1: [(bias_sums, 0), (table_sums, 0)], 2: [], 3: [(cube[1].step, 3), (cube[0].step, 3)], 5: [], 6: [(cube[2].step, 1), (small_step, 0)], 7: [(cube[1].step, 4), (cube[0].step, 4)], 9: [(small_step, 1)], 10: [(cube[2].step, 2)], 11: [(consume, 0)], 12: [(small_step, 2)], 13: [(consume, 1)], 14: [(cube[2].step, 3)], 15: [(small_step, 3)], 17: [(cube[1].step, 5), (cube[0].step, 5)]}
     cube[1].step(2)
     cube[0].step(2)
     weight_grads()

time: 209 us -> 209 us (level)
  no operation moved by 1% of the time
where the time goes in v1:
time: 209 us; the launch traced here: 208 us
  Pallas kernels  208 us (100%)
    pallas_call x1, Pallas kernels, layer(): pl.pallas_call(functools.partial(layer_kernel, bits), out_shape=shapes, i...  203 us
    pallas_call x1, Pallas kernels, finish(): pl.pallas_call(finish_kernel, out_shape=shapes, in_specs=[vm] * 6, out_sp...  4.69 us

profile of v1, /device:TPU:0, one launch (start us, length us, event | category | flops | bytes accessed | tf_op | source)
XLA Modules:
  0.0 208.5 jit_solution(4321350121782995361)
XLA Ops:
  0.7 202.9 %shard_map.410 = (f32[561,768]{1,0:T(8,128)S(1)}, f32[561,768]{1,0:T(8,128)S(1)}, f32[768,768]{1,0:T(8,128)S(1)}, f32[768,768]{1,0:T(8,128)S(1)}, f32[768,768]{1,0:T(8,128)S(1)}, /*index=5*/f32[24,768]{1,0:T(8,128)S(1)}) custom-call(f32[561,768]{1,0:T(8,128)} %tok_h.1, f32[561,768]{1,0:T(8,128)} %cot_h.1, f32[192,768]{1,0:T(8,128)} %bitcast.6, ...), custom_call_target="tpu_custom_call" | custom-call | flops 30000001024 | bytes 20971520 | tf_op jit(solution)/shard_map/pallas_call | solution.py:798
  203.6 4.7 %shard_map.411 = (f32[561,768]{1,0:T(8,128)}, f32[561,768]{1,0:T(8,128)}, f32[192,768]{1,0:T(8,128)}, f32[192,768]{1,0:T(8,128)}, f32[192,768]{1,0:T(8,128)}, /*...) custom-call(f32[561,768]{1,0:T(8,128)S(1)} %get-tuple-element.46.out, ...), custom_call_target="tpu_custom_call" | custom-call | tf_op jit(solution)/shard_map/pallas_call | solution.py:834
